TPU v7x, 512 devices: a whole 4x4x16 slice. The times are simulated.
512 devices in a mesh: grp: 32 (over y, x, core), tp: 16 (over z).
Axes of the slice: x: 4, y: 4, z: 16, core: 2. Of those that a mesh axis runs over, the one named last changes fastest.
Arguments:
- trainer_increment: float32 [1024, 128, 128], P(('tp', 'grp')), may hold values from -0.3125 to 0.3125
- trainer_residual: float32 [1024, 128, 128], P(('tp', 'grp')), may hold values from -0.3125 to 0.3125
- partition_tile_indices: int32 [512, 2], P(('tp', 'grp')), may hold values from 0 to 1, as said below
- retained_tallies: int32 [512], P(('tp', 'grp')), may hold values from 0 to 2, as said below
- projection_parameters: bfloat16 [8192, 2048], P('tp'), may hold values from -0.0625 to 0.0625
- normalized_activations: bfloat16 [4, 32, 8192], P(None, 'grp', 'tp'), may hold values from -6 to 6
- rotated_questions: bfloat16 [4, 32, 8192], P(None, 'grp'), may hold values from -256 to 256
- stored_attention_memory: bfloat16 [32, 8192, 2048], P('grp', 'tp'), may hold values from -6 to 6
- memory_fill_lengths: int32 [32], P('grp'), may hold values from 2 to 8192, as said below
Outputs:
- new_error: float32 [1024, 128, 128], P(('tp', 'grp'))
- new_kv: bfloat16 [4, 32, 2048], P(None, 'grp', 'tp')
- attention: bfloat16 [4, 32, 8192], P(None, 'grp', 'tp')
Inputs may be any that keep to these rules, and one draw needn't show every extreme that they name: `partition_tile_indices`: each row lists the local block numbers of one shard, each once; only its first retained_tallies entries name surviving blocks. `retained_tallies`: some shard lists all 2 of its blocks in every draw. Row r's valid cache positions are 0 to memory_fill_lengths[r] - 1; some row has all 8192 in every draw.
All inputs are finite; a program needn't handle non-finite values.
Results may differ from a plain program's by a relative error of at most 0.02.
Values may be sent and summed in bfloat16 or wider, within the bound.
A program may use at most 64 MiB of HBM per device.

v0:
```python
import math

import jax
import jax.numpy as jnp
from jax import lax
from jax.sharding import PartitionSpec as P

HD = 128
BLK = 128


NEG = -1e30


def merged(array, axis, combine):
    everything = jax.tree.map(lambda part: lax.all_gather(part, axis), array)
    initial = jax.tree.map(lambda part: part[0], everything)

    def step(k, so_far):
        return combine(so_far, jax.tree.map(lambda part: part[k], everything))

    return lax.fori_loop(1, lax.axis_size(axis), step, initial)


def retained_tiles(partition_tile_indices, retained_tallies):
    slots = partition_tile_indices.shape[1]
    sorting_permutation = jnp.arange(slots, dtype=jnp.int32)
    enumerated_tiles = sorting_permutation[None, :] < retained_tallies[:, None]
    hits = (
        partition_tile_indices[:, :, None] == sorting_permutation[None, None, :]
    ) & enumerated_tiles[:, :, None]
    return jnp.any(hits, axis=1)


def combine(first, second):
    top_a, total_a, blended_first = first
    top_b, total_b, mixed_b = second
    top = jnp.maximum(top_a, top_b)
    scale_a = jnp.exp(top_a - top)
    scale_b = jnp.exp(top_b - top)
    total = total_a * scale_a + total_b * scale_b
    mixed = blended_first * scale_a[..., None] + mixed_b * scale_b[..., None]
    return (top, total, mixed)


def cache_partial(rotated_questions, stored_attention_memory, memory_fill_lengths, first):
    steps, rows, width = rotated_questions.shape
    span = stored_attention_memory.shape[1]
    heads_kv = stored_attention_memory.shape[2] // (2 * HD)
    group = width // HD // heads_kv
    scale = 1.0 / math.sqrt(HD)
    query = rotated_questions.reshape(steps, rows, heads_kv, group, HD)
    cache_rows_held = stored_attention_memory.reshape(rows, span, heads_kv, 2, HD)
    scores = (
        jnp.einsum(
            "srhgd,rphd->srhgp",
            query,
            cache_rows_held[:, :, :, 0],
            preferred_element_type=jnp.float32,
        )
        * scale
    )
    position = first + jnp.arange(span, dtype=jnp.int32)
    valid = (position[None, :] < memory_fill_lengths[:, None])[None, :, None, None, :]
    scores = jnp.where(valid, scores, NEG)
    top = jnp.max(scores, axis=-1)
    probs = jnp.where(valid, jnp.exp(scores - top[..., None]), 0.0)
    total = jnp.sum(probs, axis=-1)
    values = cache_rows_held[:, :, :, 1].astype(jnp.float32)
    mixed = jnp.einsum("srhgp,rphd->srhgd", probs, values, precision=lax.Precision.HIGHEST)
    heads = heads_kv * group
    return (
        top.reshape(steps, rows, heads),
        total.reshape(steps, rows, heads),
        mixed.reshape(steps, rows, heads, HD),
    )


def body(
    trainer_increment,
    trainer_residual,
    partition_tile_indices,
    retained_tallies,
    projection_parameters,
    normalized_activations,
    rotated_questions,
    stored_attention_memory,
    memory_fill_lengths,
):
    summed = trainer_increment + trainer_residual
    retain_markers = retained_tiles(partition_tile_indices, retained_tallies).reshape(-1)
    sent = jnp.where(
        retain_markers[:, None, None], summed.astype(jnp.bfloat16), jnp.zeros((), jnp.bfloat16)
    )
    new_error = summed - sent.astype(jnp.float32)
    blocks = lax.all_gather(sent, "grp", axis=0, tiled=True)
    local_feats, kvw = projection_parameters.shape
    update = (
        blocks.reshape(local_feats // BLK, kvw // BLK, BLK, BLK)
        .transpose(0, 2, 1, 3)
        .reshape(local_feats, kvw)
    )
    patched = (projection_parameters.astype(jnp.float32) + update.astype(jnp.float32)).astype(
        jnp.bfloat16
    )
    steps, local_rows, width = normalized_activations.shape
    partial_kv = jnp.dot(
        normalized_activations.reshape(steps * local_rows, width),
        patched,
        preferred_element_type=jnp.float32,
    )
    ranks = lax.axis_size("tp")
    rank = lax.axis_index("tp")
    columns = kvw // ranks
    kv_full = lax.psum(partial_kv, "tp").astype(jnp.bfloat16)
    kv_own = lax.dynamic_slice_in_dim(kv_full, rank * columns, columns, 1)
    new_kv = kv_own.reshape(steps, local_rows, columns)
    span = stored_attention_memory.shape[1]
    top, total, mixed = cache_partial(
        rotated_questions, stored_attention_memory, memory_fill_lengths, rank * span
    )
    heads = top.shape[2]
    own = heads // ranks
    top, total, mixed = merged((top, total, mixed), "tp", combine)
    top = lax.dynamic_slice_in_dim(top, rank * own, own, 2)
    total = lax.dynamic_slice_in_dim(total, rank * own, own, 2)
    mixed = lax.dynamic_slice_in_dim(mixed, rank * own, own, 2)
    heads_kv = kvw // (2 * HD)
    group = heads // heads_kv
    scale = 1.0 / math.sqrt(HD)
    fresh = kv_full.reshape(steps, local_rows, heads_kv, 2, HD)
    head_ids = (rank * own + jnp.arange(own, dtype=jnp.int32)) // group
    fresh = jnp.take(fresh, head_ids, axis=2)
    query = lax.dynamic_slice_in_dim(rotated_questions, rank * own * HD, own * HD, 2).reshape(
        steps, local_rows, own, HD
    )
    scores = (
        jnp.einsum("srjd,urjd->srju", query, fresh[:, :, :, 0], preferred_element_type=jnp.float32)
        * scale
    )
    step_ids = jnp.arange(steps, dtype=jnp.int32)
    causal = (step_ids[None, :] <= step_ids[:, None])[:, None, None, :]
    scores = jnp.where(causal, scores, NEG)
    peak = jnp.maximum(top, jnp.max(scores, axis=-1))
    probs = jnp.where(causal, jnp.exp(scores - peak[..., None]), 0.0)
    carried = jnp.exp(top - peak)
    denom = total * carried + jnp.sum(probs, axis=-1)
    values = fresh[:, :, :, 1].astype(jnp.float32)
    numer = mixed * carried[..., None] + jnp.einsum(
        "srju,urjd->srjd", probs, values, precision=lax.Precision.HIGHEST
    )
    attention = (numer / denom[..., None]).reshape(steps, local_rows, own * HD).astype(jnp.bfloat16)
    return (new_error, new_kv, attention)


def solution(mesh):
    placed = (
        P(("tp", "grp"), None, None),
        P(("tp", "grp"), None, None),
        P(("tp", "grp"), None),
        P(("tp", "grp")),
        P("tp", None),
        P(None, "grp", "tp"),
        P(None, "grp", None),
        P("grp", "tp", None),
        P("grp"),
    )
    return jax.shard_map(
        body,
        mesh=mesh,
        in_specs=placed,
        out_specs=(P(("tp", "grp"), None, None), P(None, "grp", "tp"), P(None, "grp", "tp")),
        check_vma=False,
    )
```

profile of v0, /device:TPU:2, one launch (start us, length us, event | category | flops | bytes accessed | tf_op | source)
XLA Modules:
  0.0 221.9 jit_solution(10214104289567611357)
XLA Ops:
  7.2 2.9 %copy.91 = bf16[1,512,2048]{1,2,0:T(8,128)(2,1)S(1)} copy(bf16[1,512,2048]{2,1,0:T(8,128)(2,1)} %param.18) | data formatting | bytes 4194304 | tf_op args[7]
  11.2 1.1 convolution_bitcast_fusion.1
  15.7 35.6 %all_gather.13 = f32[16,4,1,64]{3,1,2,0:T(4,128)S(1)} all-gather(f32[1,4,1,64]{3,1,2,0:T(4,128)S(1)} %all_gather_reshape.9), channel_id=1, replica_groups=mesh['grp'=32,'tp'=16] {'tp'}, dimensions={0}, use_global_device_ids=true | all-gather | bytes 17408 | tf_op jit(solution)/shard_map/all_gather | solution.py:16
  51.4 26.1 %all_gather.14 = f32[16,4,1,64]{3,1,2,0:T(4,128)S(1)} all-gather(f32[1,4,1,64]{3,1,2,0:T(4,128)S(1)} %all_gather_reshape.10), channel_id=1, replica_groups=mesh['grp'=32,'tp'=16] {'tp'}, dimensions={0}, use_global_device_ids=true | all-gather | bytes 17408 | tf_op jit(solution)/shard_map/all_gather | solution.py:16
  77.5 13.1 %all-gather.5.cloned.1.call-done = f32[16,4,1,64,128]{4,3,2,1,0:T(8,128)} async-done(((f32[1,4,1,64,128]{4,3,2,1,0:T(8,128)}), f32[16,4,1,64,128]{4,3,2,1,0:T(8,128)}) %all-gather.5.cloned.1.call-update) | async-done | bytes 2097168 | tf_op jit(solution)/shard_map/all_gather | solution.py:16
  91.5 17.1 %while.19 = (s32[]{:T(128)}, f32[4,1,64]{2,1,0:T(1,128)S(1)}, f32[4,1,64]{2,1,0:T(1,128)S(1)}, f32[4,1,64,128]{3,2,1,0:T(8,128)S(1)}, f32[16,4,1,64]{3,1,2,0:T(4...) while((s32[]{:T(128)}, f32[4,1,64]{2,1,0:T(1,128)S(1)}, ...), condition=%wide.region_5.6_spmd, body=%wide.region_4.5_spmd.sunk | while | flops 99845 | bytes 407703 | solution.py:22
  91.5 1.1 fusion.37
  92.7 1.1 fusion.37
  93.8 1.1 fusion.37
  94.9 1.1 fusion.37
  96.1 1.1 fusion.37
  97.2 1.1 fusion.37
  98.4 1.1 fusion.37
  99.5 1.1 fusion.37
  100.6 1.1 fusion.37
  101.8 1.1 fusion.37
  102.9 1.1 fusion.37
  104.1 1.1 fusion.37
  107.5 1.1 fusion.37
  108.7 40.8 %all-gather.3.cloned.1.call-done = bf16[64,128,128]{2,1,0:T(8,128)(2,1)} async-done(((bf16[2,128,128]{2,1,0:T(8,128)(2,1)}), bf16[64,128,128]{2,1,0:T(8,128)(2,1)}) %all-gather.3.cloned.1.call-update) | async-done | bytes 2097168 | tf_op jit(solution)/shard_map/all_gather | solution.py:96
  149.5 2.1 convert_bitcast_fusion
  151.6 2.4 %copy.90 = f32[4,128,16,128]{3,2,1,0:T(8,128)S(1)} copy(f32[4,128,16,128]{3,1,2,0:T(8,128)S(1)} %convert_bitcast_fusion) | data formatting | bytes 8388608 | tf_op jit(solution)/shard_map/convert_element_type | solution.py:103
  154.1 1.3 convolution_bitcast_fusion
  155.4 56.9 %psum.7 = bf16[4,2048]{1,0:T(4,128)(2,1)S(1)} all-reduce(f32[4,2048]{1,0:T(4,128)S(1)} %convolution_bitcast_fusion), channel_id=1, replica_groups=mesh['grp'=32,'tp'=16] {'tp'}, use_global_device_ids=true, to_apply=%region_1.2 | all-reduce | flops 8192 | bytes 49152 | tf_op jit(solution)/shard_map/psum | solution.py:115
  (81 shorter events, 9.7 us)
Async XLA Ops:
  7.2 146.9 %copy-start = (bf16[4,1,512]{2,0,1:T(4,128)(2,1)S(1)}, bf16[4,1,512]{2,0,1:T(4,128)(2,1)}, u32[]{:S(2)}) copy-start(bf16[4,1,512]{2,0,1:T(4,128)(2,1)} %param.16) | copy-start | bytes 12292
  7.2 83.4 %all-gather.5.cloned.1.call-start = ((), (), s32[]{:S(2)}) async-start(), calls=%async_computation.1 | async-start | bytes 2228224 | tf_op jit(solution)/shard_map/all_gather | solution.py:16
  7.2 3.6 %copy-start.4 = (bf16[4,1,8192]{2,0,1:T(4,128)(2,1)S(1)}, bf16[4,1,8192]{2,0,1:T(4,128)(2,1)}, u32[]{:S(2)}) copy-start(bf16[4,1,8192]{2,0,1:T(4,128)(2,1)} %param.17) | copy-start | bytes 196612
  10.8 3.0 %copy-start.5 = (s32[1,2]{1,0:T(1,128)S(1)}, s32[1,2]{1,0:T(1,128)}, u32[]{:S(2)}) copy-start(s32[1,2]{1,0:T(1,128)} %param.13) | copy-start | bytes 28
  10.8 3.0 %copy-start.2 = (f32[2,128,128]{2,1,0:T(8,128)S(1)}, f32[2,128,128]{2,1,0:T(8,128)}, u32[]{:S(2)}) copy-start(f32[2,128,128]{2,1,0:T(8,128)} %param.11) | copy-start | bytes 393220
  10.8 3.0 %copy-start.3 = (f32[2,128,128]{2,1,0:T(8,128)S(1)}, f32[2,128,128]{2,1,0:T(8,128)}, u32[]{:S(2)}) copy-start(f32[2,128,128]{2,1,0:T(8,128)} %param.12) | copy-start | bytes 393220
  13.1 136.4 %all-gather.3.cloned.1.call-start = ((), (), s32[]{:S(2)}) async-start(), calls=%async_computation | async-start | bytes 2162688 | tf_op jit(solution)/shard_map/all_gather | solution.py:96
  151.6 2.5 %copy-start.1 = (bf16[512,2048]{1,0:T(8,128)(2,1)S(1)}, bf16[512,2048]{1,0:T(8,128)(2,1)}, u32[]{:S(2)}) copy-start(bf16[512,2048]{1,0:T(8,128)(2,1)} %param.15) | copy-start | bytes 6291460
Sparse Core Ops, SparseCore 0:
  13.2 77.3 all-gather.4
  93.7 55.7 all-gather.2
where the time goes:
time: 222 us
  blocking collectives  119 us (54%)
  waiting for transfers between devices  53.9 us (24%)
  other arithmetic  20.7 us (9%)
  between operations  15.5 us (7%)
  local copies, waits for them, and re-layouts  8.93 us (4%)
  matrix products  3.81 us (2%)
    all_gather x2, blocking collectives, merged(): everything = jax.tree.map(lambda part: lax.all_gather(part, axis), array)  61.6 us
    psum x1, blocking collectives, body(): kv_full = lax.psum(partial_kv, 'tp').astype(jnp.bfloat16)  56.9 us
    all_gather x1, waiting for transfers between devices, body(): blocks = lax.all_gather(sent, 'grp', axis=0, tiled=True)  40.8 us
    add x15, other arithmetic, combine(): mixed = blended_first * scale_a[..., None] + mixed_b * scale_b[..., None]  16.1 us
    all_gather x1, waiting for transfers between devices, merged(): everything = jax.tree.map(lambda part: lax.all_gather(part, axis), array)  13.1 us
  transfers between devices with their start and end apart: 2, of which 2 were waited for; matrix products, arithmetic and copies ran while one was open for 9% of the time, Pallas kernels for 0%

commit v1 on v0

v1 whole, which is shorter than its diff:
```python
import functools
import math

import jax
import jax.numpy as jnp
from jax import lax
from jax.experimental import pallas as pl
from jax.experimental.pallas import tpu as pltpu
from jax.sharding import PartitionSpec as P

HD = 128
BLK = 128
NEG = -1e30
F32 = jnp.float32
BF16 = jnp.bfloat16
MESH = pl.DeviceIdType.MESH


def remote(src, dst, send, recv, device):
    return pltpu.make_async_remote_copy(
        src_ref=src, dst_ref=dst, send_sem=send, recv_sem=recv, device_id=device, device_id_type=MESH
    )


def kernel(
    dims,
    idx_ref,
    tally_ref,
    fill_ref,
    inc_ref,
    res_ref,
    proj_ref,
    x_ref,
    q_ref,
    cache_ref,
    err_ref,
    kv_ref,
    attn_ref,
    inc_v,
    res_v,
    proj_v,
    q_v,
    cache_v,
    qf,
    wbuf,
    xbuf,
    xf,
    zsend,
    zrecv,
    kvr,
    msend,
    mrecv,
    ssend,
    srecv,
    sf,
    err_v,
    in_sem,
    cache_sem,
    err_sem,
    w_send,
    w_recv,
    x_send,
    x_recv,
    z_send,
    z_recv,
    k_send,
    k_recv,
    m_send,
    m_recv,
    s_send,
    s_recv,
):
    ny, nx, nt, steps = dims
    g = lax.axis_index("grp")
    t = lax.axis_index("tp")
    y, h = g // nx, g % nx
    span = cache_ref.shape[0]
    group = q_ref.shape[1] // HD // nx
    scale = 1.0 / math.sqrt(HD)

    barrier = pltpu.get_barrier_semaphore()
    for k in range(1, nt):
        pl.semaphore_signal(barrier, inc=1, device_id=(g, (t + k) % nt), device_id_type=MESH)
    for k in range(1, nx):
        pl.semaphore_signal(barrier, inc=1, device_id=(y * nx + (h + k) % nx, t), device_id_type=MESH)
    for k in range(1, ny):
        pl.semaphore_signal(barrier, inc=1, device_id=(((y + k) % ny) * nx + h, t), device_id_type=MESH)

    loads = [
        pltpu.make_async_copy(inc_ref, inc_v, in_sem.at[0]),
        pltpu.make_async_copy(res_ref, res_v, in_sem.at[1]),
        pltpu.make_async_copy(
            proj_ref.at[pl.ds(pl.multiple_of(y * BLK, BLK), BLK), pl.ds(pl.multiple_of(h * 2 * HD, 2 * HD), 2 * HD)],
            proj_v,
            in_sem.at[2],
        ),
        pltpu.make_async_copy(x_ref, xbuf.at[h], in_sem.at[3]),
        pltpu.make_async_copy(q_ref, q_v, in_sem.at[4]),
    ]
    for copy in loads:
        copy.start()
    cache_loads = []
    for n in range(nx):
        cols = slice(n * 2 * HD, (n + 1) * 2 * HD)
        copy = pltpu.make_async_copy(cache_ref.at[:, cols], cache_v.at[:, cols], cache_sem.at[n])
        copy.start()
        cache_loads.append(copy)

    first, second, count = idx_ref[0, 0], idx_ref[0, 1], tally_ref[0]
    for copy in loads[:3]:
        copy.wait()
    rows = pl.ds(pl.multiple_of(y * BLK, BLK), BLK)
    for j in range(2):
        keep = ((count > 0) & (first == j)) | ((count > 1) & (second == j))
        summed = inc_v[j] + res_v[j]
        sent = jnp.where(keep, summed.astype(BF16).astype(F32), 0.0)
        err_v[j] = summed - sent
        cols = slice(j * BLK, (j + 1) * BLK)
        wbuf[rows, cols] = (proj_v[:, cols].astype(F32) + sent).astype(BF16)
    err_copy = pltpu.make_async_copy(err_v, err_ref, err_sem)
    err_copy.start()

    loads[4].wait()
    for n in range(nx * group):
        qf[n * steps : (n + 1) * steps, :] = q_v[:, n * HD : (n + 1) * HD].astype(F32)

    half = group * steps // 2
    position = t * span + lax.broadcasted_iota(jnp.int32, (1, span), 1)
    valid = position < fill_ref[0]
    lane = lax.broadcasted_iota(jnp.int32, (2 * half, HD), 1)
    stats = jnp.zeros((2 * half, HD), F32)
    for n in range(nx):
        cache_loads[n].wait()
        query = qf[n * 2 * half : (n + 1) * 2 * half, :].astype(BF16)
        keys = cache_v[:, n * 2 * HD : n * 2 * HD + HD]
        values = cache_v[:, n * 2 * HD + HD : (n + 1) * 2 * HD]
        scores = lax.dot_general(query, keys, (((1,), (1,)), ((), ())), preferred_element_type=F32) * scale
        scores = jnp.where(valid, scores, NEG)
        top = jnp.max(scores, axis=1, keepdims=True)
        probs = jnp.where(valid, jnp.exp(scores - top), 0.0)
        total = jnp.sum(probs, axis=1, keepdims=True)
        mixed = jnp.dot(probs.astype(BF16), values, preferred_element_type=F32).astype(BF16)
        for i in range(2):
            part = slice(i * half, (i + 1) * half)
            msend[2 * n + i] = mixed[part]
            column = jnp.concatenate([top[part], total[part]], axis=0)
            stats = jnp.where(lane == 2 * n + i, column, stats)
    square = jnp.concatenate([stats, jnp.zeros((HD - 2 * half, HD), F32)], axis=0)
    flipped = square.T
    for n in range(nt):
        ssend[n] = flipped[n : n + 1, :]
    mrecv[t] = msend[t]
    srecv[t] = ssend[t]

    loads[3].wait()
    pl.semaphore_wait(barrier, nt + nx + ny - 3)

    w_copies = []
    for k in range(1, ny):
        copy = remote(
            wbuf.at[rows], wbuf.at[rows], w_send.at[k], w_recv.at[y], (((y + k) % ny) * nx + h, t)
        )
        copy.start()
        w_copies.append(copy)
    x_copies = []
    for k in range(1, nx):
        copy = remote(xbuf.at[h], xbuf.at[h], x_send.at[k], x_recv.at[h], (y * nx + (h + k) % nx, t))
        copy.start()
        x_copies.append(copy)

    def far(i):
        return (t + nt // 2 + ((i + 1) // 2) * (1 - 2 * (i % 2))) % nt

    def send_partials(i, carry):
        d = far(i)
        remote(msend.at[d], mrecv.at[t], m_send.at[d], m_recv.at[t], (g, d)).start()
        remote(ssend.at[d], srecv.at[t], s_send.at[d], s_recv.at[t], (g, d)).start()
        return carry

    lax.fori_loop(0, nt - 1, send_partials, 0)

    for k in range(1, nx):
        o = (h + k) % nx
        remote(xbuf.at[o], xbuf.at[o], x_send.at[k], x_recv.at[o], (g, t)).wait_recv()
    for n in range(nx):
        xf[n * steps : (n + 1) * steps, :] = xbuf[n].astype(F32)
    for k in range(1, ny):
        o = (y + k) % ny
        there = pl.ds(pl.multiple_of(o * BLK, BLK), BLK)
        remote(wbuf.at[there], wbuf.at[there], w_send.at[k], w_recv.at[o], (g, t)).wait_recv()
    product = jnp.dot(xf[...].astype(BF16), wbuf[...], preferred_element_type=F32)
    for n in range(nx):
        zsend[n, :steps, :] = product[n * steps : (n + 1) * steps, :HD]
        zsend[n, steps:, :] = product[n * steps : (n + 1) * steps, HD:]
    zrecv[h] = zsend[h]

    z_copies = []
    for k in range(1, nx):
        o = (h + k) % nx
        copy = remote(zsend.at[o], zrecv.at[h], z_send.at[k], z_recv.at[h], (y * nx + o, t))
        copy.start()
        z_copies.append(copy)

    def wait_partials(i, carry):
        d = far(i)
        remote(msend.at[d], mrecv.at[d], m_send.at[d], m_recv.at[d], (g, d)).wait_recv()
        remote(ssend.at[d], srecv.at[d], s_send.at[d], s_recv.at[d], (g, d)).wait_recv()
        return carry

    for k in range(1, nx):
        o = (h + k) % nx
        remote(zsend.at[o], zrecv.at[o], z_send.at[k], z_recv.at[o], (g, t)).wait_recv()

    kvr[t] = zrecv[t // 2]

    def send_sums(i, carry):
        d = far(i)
        remote(zrecv.at[d // 2], kvr.at[t], k_send.at[d], k_recv.at[t], (g, d)).start()
        return carry

    lax.fori_loop(0, nt - 1, send_sums, 0)

    lax.fori_loop(0, nt - 1, wait_partials, 0)
    for n in range(nt):
        sf[n : n + 1, :] = srecv[n]
    s_all = sf[...]
    peak_all = jnp.max(s_all, axis=0, keepdims=True)
    weight = jnp.exp(s_all - peak_all)
    total_all = jnp.sum(weight * pltpu.roll(s_all, HD - half, 1), axis=0, keepdims=True)
    table = jnp.concatenate(
        [weight, total_all, peak_all, jnp.zeros((HD - nt - 2, HD), F32)], axis=0
    ).T[:half]
    numer = jnp.zeros((half, HD), F32)
    for n in range(nt):
        numer = numer + table[:, n : n + 1] * mrecv[n].astype(F32)
    total = table[:, nt : nt + 1]
    top = table[:, nt + 1 : nt + 2]
    query = qf[pl.ds(pl.multiple_of(t * half, half), half), :]
    step = lax.broadcasted_iota(jnp.int32, (half, 1), 0) % steps

    def wait_sums(i, carry):
        d = far(i)
        remote(kvr.at[d], kvr.at[d], k_send.at[d], k_recv.at[d], (g, d)).wait_recv()
        return carry

    lax.fori_loop(0, nt - 1, wait_sums, 0)
    fresh = kvr[0]
    for n in range(1, nt):
        fresh = fresh + kvr[n]
    rounded = fresh.astype(BF16).astype(F32)
    kv_ref[...] = jnp.where(t % 2 == 0, rounded[:steps], rounded[steps:]).astype(BF16)
    scores = []
    for u in range(steps):
        s = jnp.sum(query * rounded[u : u + 1, :], axis=1, keepdims=True) * scale
        scores.append(jnp.where(step >= u, s, NEG))
    peak = top
    for s in scores:
        peak = jnp.maximum(peak, s)
    carried = jnp.exp(top - peak)
    denom = total * carried
    numer = numer * carried
    for u in range(steps):
        p = jnp.where(step >= u, jnp.exp(scores[u] - peak), 0.0)
        denom = denom + p
        numer = numer + p * rounded[steps + u : steps + u + 1, :]
    result = numer / denom
    for n in range(half // steps):
        attn_ref[:, n * HD : (n + 1) * HD] = result[n * steps : (n + 1) * steps, :].astype(BF16)

    err_copy.wait()
    for copy in w_copies + x_copies + z_copies:
        copy.wait_send()

    def drain(i, carry):
        d = far(i)
        remote(msend.at[d], mrecv.at[d], m_send.at[d], m_recv.at[d], (g, d)).wait_send()
        remote(ssend.at[d], srecv.at[d], s_send.at[d], s_recv.at[d], (g, d)).wait_send()
        remote(kvr.at[d], kvr.at[d], k_send.at[d], k_recv.at[d], (g, d)).wait_send()
        return carry

    lax.fori_loop(0, nt - 1, drain, 0)


def body(
    trainer_increment,
    trainer_residual,
    partition_tile_indices,
    retained_tallies,
    projection_parameters,
    normalized_activations,
    rotated_questions,
    stored_attention_memory,
    memory_fill_lengths,
):
    local_feats, kvw = projection_parameters.shape
    ny = local_feats // BLK
    nx = kvw // (2 * HD)
    nt = lax.axis_size("tp")
    steps = normalized_activations.shape[0]
    span = stored_attention_memory.shape[1]
    qwidth = rotated_questions.shape[2]
    half = qwidth // HD // nx * steps // 2
    hbm = pl.BlockSpec(memory_space=pl.ANY)
    vmem = pl.BlockSpec(memory_space=pltpu.VMEM)
    smem = pl.BlockSpec(memory_space=pltpu.SMEM)
    dma = pltpu.SemaphoreType.DMA
    new_error, new_kv, attention = pl.pallas_call(
        functools.partial(kernel, (ny, nx, nt, steps)),
        out_shape=(
            jax.ShapeDtypeStruct(trainer_increment.shape, F32),
            jax.ShapeDtypeStruct((steps, kvw // nt), BF16),
            jax.ShapeDtypeStruct((steps, qwidth // nt), BF16),
        ),
        in_specs=[smem, smem, smem, hbm, hbm, hbm, hbm, hbm, hbm],
        out_specs=(hbm, vmem, vmem),
        scratch_shapes=[
            pltpu.VMEM((2, BLK, BLK), F32),
            pltpu.VMEM((2, BLK, BLK), F32),
            pltpu.VMEM((BLK, 2 * HD), BF16),
            pltpu.VMEM((steps, qwidth), BF16),
            pltpu.VMEM((span, kvw), BF16),
            pltpu.VMEM((qwidth // HD * steps, HD), F32),
            pltpu.VMEM((local_feats, 2 * HD), BF16),
            pltpu.VMEM((nx, steps, local_feats), BF16),
            pltpu.VMEM((nx * steps, local_feats), F32),
            pltpu.VMEM((nx, 2 * steps, HD), F32),
            pltpu.VMEM((nx, 2 * steps, HD), F32),
            pltpu.VMEM((nt, 2 * steps, HD), F32),
            pltpu.VMEM((nt, half, HD), BF16),
            pltpu.VMEM((nt, half, HD), BF16),
            pltpu.VMEM((nt, 1, HD), F32),
            pltpu.VMEM((nt, 1, HD), F32),
            pltpu.VMEM((nt, HD), F32),
            pltpu.VMEM((2, BLK, BLK), F32),
            dma((5,)),
            dma((nx,)),
            dma,
            dma((ny,)),
            dma((ny,)),
            dma((nx,)),
            dma((nx,)),
            dma((nx,)),
            dma((nx,)),
            dma((nt,)),
            dma((nt,)),
            dma((nt,)),
            dma((nt,)),
            dma((nt,)),
            dma((nt,)),
        ],
        compiler_params=pltpu.CompilerParams(collective_id=0, has_side_effects=True),
    )(
        partition_tile_indices,
        retained_tallies,
        memory_fill_lengths,
        trainer_increment,
        trainer_residual,
        projection_parameters,
        normalized_activations.reshape(steps, local_feats),
        rotated_questions.reshape(steps, qwidth),
        stored_attention_memory.reshape(span, kvw),
    )
    return (
        new_error,
        new_kv.reshape(steps, 1, kvw // nt),
        attention.reshape(steps, 1, qwidth // nt),
    )


def solution(mesh):
    placed = (
        P(("tp", "grp"), None, None),
        P(("tp", "grp"), None, None),
        P(("tp", "grp"), None),
        P(("tp", "grp")),
        P("tp", None),
        P(None, "grp", "tp"),
        P(None, "grp", None),
        P("grp", "tp", None),
        P("grp"),
    )
    return jax.shard_map(
        body,
        mesh=mesh,
        in_specs=placed,
        out_specs=(P(("tp", "grp"), None, None), P(None, "grp", "tp"), P(None, "grp", "tp")),
        check_vma=False,
    )
```

time: 222 us -> 42.6 us (0.19)
  the two profiles are of different devices: /device:TPU:2 before, /device:TPU:1 now
where the time goes in v1:
time: 42.6 us; the launch traced here: 42.4 us
  Pallas kernels  36.4 us (85%)
  local copies, waits for them, and re-layouts  4.06 us (10%)
  between operations  1.93 us (5%)
    pallas_call x1, Pallas kernels, body(): pl.pallas_call(functools.partial(kernel, (ny, nx, nt, steps)), out_shape=...  36.4 us
    unnamed x3, local copies, waits for them, and re-layouts  4.06 us

profile of v1, /device:TPU:1, one launch (start us, length us, event | category | flops | bytes accessed | tf_op | source)
XLA Modules:
  0.0 42.4 jit_solution(11530026586420581807)
XLA Ops:
  1.9 36.4 %shard_map.112 = (f32[2,128,128]{2,1,0:T(8,128)}, bf16[4,128]{1,0:T(4,128)(2,1)}, bf16[4,512]{1,0:T(4,128)(2,1)}) custom-call(s32[1,2]{1,0:T(1,128)} %idx_ref.1, s32[1]{0:T(128)S(6)} %copy.15.tally_ref, s32[1]{0:T(128)S(6)} %copy.16.fill_ref, f32[2,128,128]{2,1,0:T(8,128)} %inc_ref.1, f32[2,128,128]{2,1,0:T(8,128)} %res_ref.1, bf16[512,2048]{1,0:T(8,128)(2,1)} %proj_ref.1, ...), custom_call_target="tpu_custom_call" | custom-call | tf_op jit(solution)/shard_map/pallas_call | solution.py:307
  38.3 1.6 %copy.17 = f32[2,128,128]{2,1,0:T(8,128)} copy(f32[2,128,128]{2,1,0:T(8,128)} %get-tuple-element.12) | data formatting | bytes 262144
  39.9 1.2 %copy.18 = bf16[4,1,128]{2,0,1:T(4,128)(2,1)} copy(bf16[4,1,128]{2,0,1:T(4,128)(2,1)} %bitcast.9) | data formatting | bytes 2048
  41.1 1.3 %copy.19 = bf16[4,1,512]{2,0,1:T(4,128)(2,1)} copy(bf16[4,1,512]{2,0,1:T(4,128)(2,1)} %bitcast.8) | data formatting | bytes 8192

commit v2 on v1

--- a/solution.py
+++ b/solution.py
@@ -24,9 +24,9 @@
 
 def kernel(
     dims,
-    idx_ref,
-    tally_ref,
-    fill_ref,
+    idx_hbm,
+    tally_hbm,
+    fill_hbm,
     inc_ref,
     res_ref,
     proj_ref,
@@ -36,6 +36,9 @@
     err_ref,
     kv_ref,
     attn_ref,
+    idx_ref,
+    tally_ref,
+    fill_ref,
     inc_v,
     res_v,
     proj_v,
@@ -53,10 +56,8 @@
     ssend,
     srecv,
     sf,
-    err_v,
     in_sem,
     cache_sem,
-    err_sem,
     w_send,
     w_recv,
     x_send,
@@ -96,6 +97,9 @@
         ),
         pltpu.make_async_copy(x_ref, xbuf.at[h], in_sem.at[3]),
         pltpu.make_async_copy(q_ref, q_v, in_sem.at[4]),
+        pltpu.make_async_copy(idx_hbm, idx_ref, in_sem.at[5]),
+        pltpu.make_async_copy(tally_hbm, tally_ref, in_sem.at[6]),
+        pltpu.make_async_copy(fill_hbm, fill_ref, in_sem.at[7]),
     ]
     for copy in loads:
         copy.start()
@@ -106,19 +110,31 @@
         copy.start()
         cache_loads.append(copy)
 
+    for copy in loads[:4] + loads[5:]:
+        copy.wait()
     first, second, count = idx_ref[0, 0], idx_ref[0, 1], tally_ref[0]
-    for copy in loads[:3]:
-        copy.wait()
     rows = pl.ds(pl.multiple_of(y * BLK, BLK), BLK)
     for j in range(2):
         keep = ((count > 0) & (first == j)) | ((count > 1) & (second == j))
         summed = inc_v[j] + res_v[j]
         sent = jnp.where(keep, summed.astype(BF16).astype(F32), 0.0)
-        err_v[j] = summed - sent
+        err_ref[j] = summed - sent
         cols = slice(j * BLK, (j + 1) * BLK)
         wbuf[rows, cols] = (proj_v[:, cols].astype(F32) + sent).astype(BF16)
-    err_copy = pltpu.make_async_copy(err_v, err_ref, err_sem)
-    err_copy.start()
+    pl.semaphore_wait(barrier, nt + nx + ny - 3)
+
+    w_copies = []
+    for k in range(1, ny):
+        copy = remote(
+            wbuf.at[rows], wbuf.at[rows], w_send.at[k], w_recv.at[y], (((y + k) % ny) * nx + h, t)
+        )
+        copy.start()
+        w_copies.append(copy)
+    x_copies = []
+    for k in range(1, nx):
+        copy = remote(xbuf.at[h], xbuf.at[h], x_send.at[k], x_recv.at[h], (y * nx + (h + k) % nx, t))
+        copy.start()
+        x_copies.append(copy)
 
     loads[4].wait()
     for n in range(nx * group):
@@ -152,22 +168,6 @@
     mrecv[t] = msend[t]
     srecv[t] = ssend[t]
 
-    loads[3].wait()
-    pl.semaphore_wait(barrier, nt + nx + ny - 3)
-
-    w_copies = []
-    for k in range(1, ny):
-        copy = remote(
-            wbuf.at[rows], wbuf.at[rows], w_send.at[k], w_recv.at[y], (((y + k) % ny) * nx + h, t)
-        )
-        copy.start()
-        w_copies.append(copy)
-    x_copies = []
-    for k in range(1, nx):
-        copy = remote(xbuf.at[h], xbuf.at[h], x_send.at[k], x_recv.at[h], (y * nx + (h + k) % nx, t))
-        copy.start()
-        x_copies.append(copy)
-
     def far(i):
         return (t + nt // 2 + ((i + 1) // 2) * (1 - 2 * (i % 2))) % nt
 
@@ -267,7 +267,6 @@
     for n in range(half // steps):
         attn_ref[:, n * HD : (n + 1) * HD] = result[n * steps : (n + 1) * steps, :].astype(BF16)
 
-    err_copy.wait()
     for copy in w_copies + x_copies + z_copies:
         copy.wait_send()
 
@@ -279,6 +278,18 @@
         return carry
 
     lax.fori_loop(0, nt - 1, drain, 0)
+
+
+def put_out(err_ref, kv_ref, attn_ref, err_out, kv_out, attn_out, sem):
+    copies = [
+        pltpu.make_async_copy(err_ref, err_out, sem.at[0]),
+        pltpu.make_async_copy(kv_ref, kv_out, sem.at[1]),
+        pltpu.make_async_copy(attn_ref, attn_out, sem.at[2]),
+    ]
+    for copy in copies:
+        copy.start()
+    for copy in copies:
+        copy.wait()
 
 
 def body(
@@ -300,20 +311,23 @@
     span = stored_attention_memory.shape[1]
     qwidth = rotated_questions.shape[2]
     half = qwidth // HD // nx * steps // 2
-    hbm = pl.BlockSpec(memory_space=pl.ANY)
+    hbm = pl.BlockSpec(memory_space=pltpu.HBM)
+    anywhere = pl.BlockSpec(memory_space=pl.ANY)
     vmem = pl.BlockSpec(memory_space=pltpu.VMEM)
-    smem = pl.BlockSpec(memory_space=pltpu.SMEM)
     dma = pltpu.SemaphoreType.DMA
     new_error, new_kv, attention = pl.pallas_call(
         functools.partial(kernel, (ny, nx, nt, steps)),
         out_shape=(
-            jax.ShapeDtypeStruct(trainer_increment.shape, F32),
-            jax.ShapeDtypeStruct((steps, kvw // nt), BF16),
-            jax.ShapeDtypeStruct((steps, qwidth // nt), BF16),
+            pltpu.VMEM(trainer_increment.shape, F32),
+            pltpu.VMEM((steps, kvw // nt), BF16),
+            pltpu.VMEM((steps, qwidth // nt), BF16),
         ),
-        in_specs=[smem, smem, smem, hbm, hbm, hbm, hbm, hbm, hbm],
-        out_specs=(hbm, vmem, vmem),
+        in_specs=[hbm, hbm, hbm, hbm, hbm, hbm, hbm, hbm, hbm],
+        out_specs=(vmem, vmem, vmem),
         scratch_shapes=[
+            pltpu.SMEM((1, 2), jnp.int32),
+            pltpu.SMEM((1,), jnp.int32),
+            pltpu.SMEM((1,), jnp.int32),
             pltpu.VMEM((2, BLK, BLK), F32),
             pltpu.VMEM((2, BLK, BLK), F32),
             pltpu.VMEM((BLK, 2 * HD), BF16),
@@ -331,10 +345,8 @@
             pltpu.VMEM((nt, 1, HD), F32),
             pltpu.VMEM((nt, 1, HD), F32),
             pltpu.VMEM((nt, HD), F32),
-            pltpu.VMEM((2, BLK, BLK), F32),
-            dma((5,)),
+            dma((8,)),
             dma((nx,)),
-            dma,
             dma((ny,)),
             dma((ny,)),
             dma((nx,)),
@@ -360,6 +372,14 @@
         rotated_questions.reshape(steps, qwidth),
         stored_attention_memory.reshape(span, kvw),
     )
+    outs = (new_error, new_kv, attention)
+    new_error, new_kv, attention = pl.pallas_call(
+        put_out,
+        out_shape=tuple(jax.ShapeDtypeStruct(out.shape, out.dtype) for out in outs),
+        in_specs=[anywhere] * 3,
+        out_specs=(hbm,) * 3,
+        scratch_shapes=[dma((3,))],
+    )(*(pltpu.with_memory_space_constraint(out, pltpu.VMEM) for out in outs))
     return (
         new_error,
         new_kv.reshape(steps, 1, kvw // nt),

time: 42.6 us -> 36.7 us (0.86)
  local copies, waits for them, and re-layouts: 4.06 us -> 0 us
  Pallas kernels: 36.4 us -> 34.6 us
    unnamed x3 -> x0, local copies, waits for them, and re-layouts: 4.06 us -> none
    pallas_call x1, Pallas kernels: 36.4 us -> 33.9 us  [body(): pl.pallas_call(functools.partial(kernel, (ny, nx, nt, steps)), out_shape=...]
    pallas_call x0 -> x1, Pallas kernels: none -> 0.69 us  [body(): pl.pallas_call(put_out, out_shape=tuple((jax.ShapeDtypeStruct(out.shape,...]
where the time goes in v2:
time: 36.7 us; the launch traced here: 36.5 us
  Pallas kernels  34.6 us (94%)
  between operations  1.93 us (5%)
    pallas_call x1, Pallas kernels, body(): pl.pallas_call(functools.partial(kernel, (ny, nx, nt, steps)), out_shape=...  33.9 us

profile of v2, /device:TPU:1, one launch (start us, length us, event | category | flops | bytes accessed | tf_op | source)
XLA Modules:
  0.0 36.5 jit_solution(12256076507047747833)
XLA Ops:
  1.9 33.9 %shard_map.112 = (f32[2,128,128]{2,1,0:T(8,128)S(1)}, bf16[4,128]{1,0:T(4,128)(2,1)S(1)}, bf16[4,512]{1,0:T(4,128)(2,1)S(1)}) custom-call(s32[1,2]{1,0:T(1,128)} %idx_hbm.1, s32[1]{0:T(128)S(6)} %copy.12.tally_hbm, s32[1]{0:T(128)S(6)} %copy.13.fill_hbm, f32[2,128,128]{2,1,0:T(8,128)} %inc_ref.1, f32[2,128,128]{2,1,0:T(8,128)} %res_ref.1, ...), custom_call_target="tpu_custom_call" | custom-call | tf_op jit(solution)/shard_map/pallas_call | solution.py:318
  35.8 0.7 %shard_map.113 = (f32[2,128,128]{2,1,0:T(8,128)}, bf16[4,128]{1,0:T(4,128)(2,1)}, bf16[4,512]{1,0:T(4,128)(2,1)}) custom-call(f32[2,128,128]{2,1,0:T(8,128)S(1)} %get-tuple-element.9.err_ref, bf16[4,128]{1,0:T(4,128)(2,1)S(1)} %get-tuple-element.10.kv_ref, bf16[4,512]{1,0:T(4,128)(2,1)S(1)} %get-tuple-element.11.attn_ref), custom_call_target="tpu_custom_call" | custom-call | tf_op jit(solution)/shard_map/pallas_call | solution.py:376

commit v3 on v2

--- a/solution.py
+++ b/solution.py
@@ -70,6 +70,7 @@
     m_recv,
     s_send,
     s_recv,
+    known,
 ):
     ny, nx, nt, steps = dims
     g = lax.axis_index("grp")
@@ -78,14 +79,6 @@
     span = cache_ref.shape[0]
     group = q_ref.shape[1] // HD // nx
     scale = 1.0 / math.sqrt(HD)
-
-    barrier = pltpu.get_barrier_semaphore()
-    for k in range(1, nt):
-        pl.semaphore_signal(barrier, inc=1, device_id=(g, (t + k) % nt), device_id_type=MESH)
-    for k in range(1, nx):
-        pl.semaphore_signal(barrier, inc=1, device_id=(y * nx + (h + k) % nx, t), device_id_type=MESH)
-    for k in range(1, ny):
-        pl.semaphore_signal(barrier, inc=1, device_id=(((y + k) % ny) * nx + h, t), device_id_type=MESH)
 
     loads = [
         pltpu.make_async_copy(inc_ref, inc_v, in_sem.at[0]),
@@ -110,6 +103,14 @@
         copy.start()
         cache_loads.append(copy)
 
+    barrier = pltpu.get_barrier_semaphore()
+    for k in (1, nt - 1):
+        pl.semaphore_signal(barrier, inc=1, device_id=(g, (t + k) % nt), device_id_type=MESH)
+    for k in range(1, nx):
+        pl.semaphore_signal(barrier, inc=1, device_id=(y * nx + (h + k) % nx, t), device_id_type=MESH)
+    for k in range(1, ny):
+        pl.semaphore_signal(barrier, inc=1, device_id=(((y + k) % ny) * nx + h, t), device_id_type=MESH)
+
     for copy in loads[:4] + loads[5:]:
         copy.wait()
     first, second, count = idx_ref[0, 0], idx_ref[0, 1], tally_ref[0]
@@ -121,7 +122,21 @@
         err_ref[j] = summed - sent
         cols = slice(j * BLK, (j + 1) * BLK)
         wbuf[rows, cols] = (proj_v[:, cols].astype(F32) + sent).astype(BF16)
-    pl.semaphore_wait(barrier, nt + nx + ny - 3)
+    pl.semaphore_wait(barrier, nx + ny)
+
+    reach = [1 << r for r in range(8) if (1 << r) < nt // 2]
+
+    def tell(r):
+        for k in (reach[r], nt - reach[r]):
+            pl.semaphore_signal(known.at[r], inc=1, device_id=(g, (t + k) % nt), device_id_type=MESH)
+
+    def learn(r):
+        if 0 <= r < len(reach):
+            pl.semaphore_wait(known.at[r], 2)
+            if r + 1 < len(reach):
+                tell(r + 1)
+
+    tell(0)
 
     w_copies = []
     for k in range(1, ny):
@@ -161,6 +176,9 @@
             msend[2 * n + i] = mixed[part]
             column = jnp.concatenate([top[part], total[part]], axis=0)
             stats = jnp.where(lane == 2 * n + i, column, stats)
+        if n == nx // 2 - 1:
+            learn(len(reach) - 3)
+    learn(len(reach) - 2)
     square = jnp.concatenate([stats, jnp.zeros((HD - 2 * half, HD), F32)], axis=0)
     flipped = square.T
     for n in range(nt):
@@ -177,7 +195,6 @@
         remote(ssend.at[d], srecv.at[t], s_send.at[d], s_recv.at[t], (g, d)).start()
         return carry
 
-    lax.fori_loop(0, nt - 1, send_partials, 0)
 
     for k in range(1, nx):
         o = (h + k) % nx
@@ -201,24 +218,33 @@
         copy.start()
         z_copies.append(copy)
 
+    learn(len(reach) - 1)
+    lax.fori_loop(0, nt - 1, send_partials, 0)
+
     def wait_partials(i, carry):
         d = far(i)
         remote(msend.at[d], mrecv.at[d], m_send.at[d], m_recv.at[d], (g, d)).wait_recv()
         remote(ssend.at[d], srecv.at[d], s_send.at[d], s_recv.at[d], (g, d)).wait_recv()
         return carry
 
-    for k in range(1, nx):
-        o = (h + k) % nx
-        remote(zsend.at[o], zrecv.at[o], z_send.at[k], z_recv.at[o], (g, t)).wait_recv()
-
+    def send_sums(i, carry):
+        o = (h + i) % nx
+
+        @pl.when(i > 0)
+        def _():
+            remote(zsend.at[o], zrecv.at[o], z_send.at[i], z_recv.at[o], (g, t)).wait_recv()
+
+        for j in range(2):
+            d = 2 * o + j
+
+            @pl.when(d != t)
+            def _():
+                remote(zrecv.at[o], kvr.at[t], k_send.at[d], k_recv.at[t], (g, d)).start()
+
+        return carry
+
+    lax.fori_loop(0, nx, send_sums, 0)
     kvr[t] = zrecv[t // 2]
-
-    def send_sums(i, carry):
-        d = far(i)
-        remote(zrecv.at[d // 2], kvr.at[t], k_send.at[d], k_recv.at[t], (g, d)).start()
-        return carry
-
-    lax.fori_loop(0, nt - 1, send_sums, 0)
 
     lax.fori_loop(0, nt - 1, wait_partials, 0)
     for n in range(nt):
@@ -359,6 +385,7 @@
             dma((nt,)),
             dma((nt,)),
             dma((nt,)),
+            pltpu.SemaphoreType.REGULAR((8,)),
         ],
         compiler_params=pltpu.CompilerParams(collective_id=0, has_side_effects=True),
     )(

time: 36.7 us -> 35.2 us (0.959)
  Pallas kernels: 34.6 us -> 32.8 us
    pallas_call x1, Pallas kernels: 33.9 us -> 32.1 us  [body(): pl.pallas_call(functools.partial(kernel, (ny, nx, nt, steps)), out_shape=...]
where the time goes in v3:
time: 35.2 us; the launch traced here: 34.7 us
  Pallas kernels  32.8 us (93%)
  between operations  1.93 us (5%)
    pallas_call x1, Pallas kernels, body(): pl.pallas_call(functools.partial(kernel, (ny, nx, nt, steps)), out_shape=...  32.1 us

profile of v3, /device:TPU:1, one launch (start us, length us, event | category | flops | bytes accessed | tf_op | source)
XLA Modules:
  0.0 34.7 jit_solution(4384131618253044069)
XLA Ops:
  1.9 32.1 %shard_map.112 = (f32[2,128,128]{2,1,0:T(8,128)S(1)}, bf16[4,128]{1,0:T(4,128)(2,1)S(1)}, bf16[4,512]{1,0:T(4,128)(2,1)S(1)}) custom-call(s32[1,2]{1,0:T(1,128)} %idx_hbm.1, s32[1]{0:T(128)S(6)} %copy.12.tally_hbm, s32[1]{0:T(128)S(6)} %copy.13.fill_hbm, f32[2,128,128]{2,1,0:T(8,128)} %inc_ref.1, f32[2,128,128]{2,1,0:T(8,128)} %res_ref.1, ...), custom_call_target="tpu_custom_call" | custom-call | tf_op jit(solution)/shard_map/pallas_call | solution.py:344
  34.0 0.7 %shard_map.113 = (f32[2,128,128]{2,1,0:T(8,128)}, bf16[4,128]{1,0:T(4,128)(2,1)}, bf16[4,512]{1,0:T(4,128)(2,1)}) custom-call(f32[2,128,128]{2,1,0:T(8,128)S(1)} %get-tuple-element.9.err_ref, bf16[4,128]{1,0:T(4,128)(2,1)S(1)} %get-tuple-element.10.kv_ref, bf16[4,512]{1,0:T(4,128)(2,1)S(1)} %get-tuple-element.11.attn_ref), custom_call_target="tpu_custom_call" | custom-call | tf_op jit(solution)/shard_map/pallas_call | solution.py:403

commit v4 on v3

--- a/solution.py
+++ b/solution.py
@@ -94,14 +94,8 @@
         pltpu.make_async_copy(tally_hbm, tally_ref, in_sem.at[6]),
         pltpu.make_async_copy(fill_hbm, fill_ref, in_sem.at[7]),
     ]
-    for copy in loads:
-        copy.start()
-    cache_loads = []
-    for n in range(nx):
-        cols = slice(n * 2 * HD, (n + 1) * 2 * HD)
-        copy = pltpu.make_async_copy(cache_ref.at[:, cols], cache_v.at[:, cols], cache_sem.at[n])
-        copy.start()
-        cache_loads.append(copy)
+    for copy in loads[:4] + loads[5:]:
+        copy.start()
 
     barrier = pltpu.get_barrier_semaphore()
     for k in (1, nt - 1):
@@ -110,6 +104,14 @@
         pl.semaphore_signal(barrier, inc=1, device_id=(y * nx + (h + k) % nx, t), device_id_type=MESH)
     for k in range(1, ny):
         pl.semaphore_signal(barrier, inc=1, device_id=(((y + k) % ny) * nx + h, t), device_id_type=MESH)
+
+    loads[4].start()
+    cache_loads = []
+    for n in range(nx):
+        cols = slice(n * 2 * HD, (n + 1) * 2 * HD)
+        copy = pltpu.make_async_copy(cache_ref.at[:, cols], cache_v.at[:, cols], cache_sem.at[n])
+        copy.start()
+        cache_loads.append(copy)
 
     for copy in loads[:4] + loads[5:]:
         copy.wait()
@@ -160,23 +162,30 @@
     valid = position < fill_ref[0]
     lane = lax.broadcasted_iota(jnp.int32, (2 * half, HD), 1)
     stats = jnp.zeros((2 * half, HD), F32)
-    for n in range(nx):
-        cache_loads[n].wait()
-        query = qf[n * 2 * half : (n + 1) * 2 * half, :].astype(BF16)
-        keys = cache_v[:, n * 2 * HD : n * 2 * HD + HD]
-        values = cache_v[:, n * 2 * HD + HD : (n + 1) * 2 * HD]
-        scores = lax.dot_general(query, keys, (((1,), (1,)), ((), ())), preferred_element_type=F32) * scale
-        scores = jnp.where(valid, scores, NEG)
-        top = jnp.max(scores, axis=1, keepdims=True)
-        probs = jnp.where(valid, jnp.exp(scores - top), 0.0)
-        total = jnp.sum(probs, axis=1, keepdims=True)
-        mixed = jnp.dot(probs.astype(BF16), values, preferred_element_type=F32).astype(BF16)
-        for i in range(2):
-            part = slice(i * half, (i + 1) * half)
-            msend[2 * n + i] = mixed[part]
-            column = jnp.concatenate([top[part], total[part]], axis=0)
-            stats = jnp.where(lane == 2 * n + i, column, stats)
-        if n == nx // 2 - 1:
+    for copy in cache_loads:
+        copy.wait()
+    for batch in (range(nx // 2), range(nx // 2, nx)):
+        parts = {}
+        for n in batch:
+            query = qf[n * 2 * half : (n + 1) * 2 * half, :].astype(BF16)
+            keys = cache_v[:, n * 2 * HD : n * 2 * HD + HD]
+            scores = lax.dot_general(query, keys, (((1,), (1,)), ((), ())), preferred_element_type=F32)
+            parts[n] = jnp.where(valid, scores * scale, NEG)
+        for n in batch:
+            scores = parts[n]
+            top = jnp.max(scores, axis=1, keepdims=True)
+            probs = jnp.where(valid, jnp.exp(scores - top), 0.0)
+            parts[n] = (top, jnp.sum(probs, axis=1, keepdims=True), probs.astype(BF16))
+        for n in batch:
+            top, total, probs = parts[n]
+            values = cache_v[:, n * 2 * HD + HD : (n + 1) * 2 * HD]
+            mixed = jnp.dot(probs, values, preferred_element_type=F32).astype(BF16)
+            for i in range(2):
+                part = slice(i * half, (i + 1) * half)
+                msend[2 * n + i] = mixed[part]
+                column = jnp.concatenate([top[part], total[part]], axis=0)
+                stats = jnp.where(lane == 2 * n + i, column, stats)
+        if batch[0] == 0:
             learn(len(reach) - 3)
     learn(len(reach) - 2)
     square = jnp.concatenate([stats, jnp.zeros((HD - 2 * half, HD), F32)], axis=0)
@@ -186,15 +195,20 @@
     mrecv[t] = msend[t]
     srecv[t] = ssend[t]
 
-    def far(i):
-        return (t + nt // 2 + ((i + 1) // 2) * (1 - 2 * (i % 2))) % nt
-
-    def send_partials(i, carry):
-        d = far(i)
-        remote(msend.at[d], mrecv.at[t], m_send.at[d], m_recv.at[t], (g, d)).start()
-        remote(ssend.at[d], srecv.at[t], s_send.at[d], s_recv.at[t], (g, d)).start()
-        return carry
-
+    near = reach[-1]
+
+    def send_partials(d, far):
+        gap = (d - t + nt) % nt
+        close = (gap <= near) | (gap >= nt - near)
+
+        @pl.when((gap > 0) & (close != far))
+        def _():
+            remote(msend.at[d], mrecv.at[t], m_send, m_recv, (g, d)).start()
+            remote(ssend.at[d], srecv.at[t], s_send, s_recv, (g, d)).start()
+
+        return far
+
+    lax.fori_loop(0, nt, send_partials, False)
 
     for k in range(1, nx):
         o = (h + k) % nx
@@ -219,34 +233,33 @@
         z_copies.append(copy)
 
     learn(len(reach) - 1)
-    lax.fori_loop(0, nt - 1, send_partials, 0)
-
-    def wait_partials(i, carry):
-        d = far(i)
-        remote(msend.at[d], mrecv.at[d], m_send.at[d], m_recv.at[d], (g, d)).wait_recv()
-        remote(ssend.at[d], srecv.at[d], s_send.at[d], s_recv.at[d], (g, d)).wait_recv()
-        return carry
+    lax.fori_loop(0, nt, send_partials, True)
 
     def send_sums(i, carry):
-        o = (h + i) % nx
-
-        @pl.when(i > 0)
+        o = i
+
+        @pl.when(o != h)
         def _():
-            remote(zsend.at[o], zrecv.at[o], z_send.at[i], z_recv.at[o], (g, t)).wait_recv()
+            remote(zsend.at[o], zrecv.at[o], z_send.at[0], z_recv.at[o], (g, t)).wait_recv()
 
         for j in range(2):
             d = 2 * o + j
 
             @pl.when(d != t)
             def _():
-                remote(zrecv.at[o], kvr.at[t], k_send.at[d], k_recv.at[t], (g, d)).start()
+                remote(zrecv.at[o], kvr.at[t], k_send, k_recv, (g, d)).start()
 
         return carry
 
     lax.fori_loop(0, nx, send_sums, 0)
     kvr[t] = zrecv[t // 2]
 
-    lax.fori_loop(0, nt - 1, wait_partials, 0)
+    others = pl.ds(0, nt - 1)
+    m_all = remote(msend.at[others], mrecv.at[others], m_send, m_recv, (g, t))
+    s_all_copies = remote(ssend.at[others], srecv.at[others], s_send, s_recv, (g, t))
+    k_all = remote(kvr.at[others], kvr.at[others], k_send, k_recv, (g, t))
+    m_all.wait_recv()
+    s_all_copies.wait_recv()
     for n in range(nt):
         sf[n : n + 1, :] = srecv[n]
     s_all = sf[...]
@@ -264,12 +277,12 @@
     query = qf[pl.ds(pl.multiple_of(t * half, half), half), :]
     step = lax.broadcasted_iota(jnp.int32, (half, 1), 0) % steps
 
-    def wait_sums(i, carry):
-        d = far(i)
-        remote(kvr.at[d], kvr.at[d], k_send.at[d], k_recv.at[d], (g, d)).wait_recv()
-        return carry
-
-    lax.fori_loop(0, nt - 1, wait_sums, 0)
+    for copy in w_copies + x_copies + z_copies:
+        copy.wait_send()
+    m_all.wait_send()
+    s_all_copies.wait_send()
+    k_all.wait_send()
+    k_all.wait_recv()
     fresh = kvr[0]
     for n in range(1, nt):
         fresh = fresh + kvr[n]
@@ -292,18 +305,6 @@
     result = numer / denom
     for n in range(half // steps):
         attn_ref[:, n * HD : (n + 1) * HD] = result[n * steps : (n + 1) * steps, :].astype(BF16)
-
-    for copy in w_copies + x_copies + z_copies:
-        copy.wait_send()
-
-    def drain(i, carry):
-        d = far(i)
-        remote(msend.at[d], mrecv.at[d], m_send.at[d], m_recv.at[d], (g, d)).wait_send()
-        remote(ssend.at[d], srecv.at[d], s_send.at[d], s_recv.at[d], (g, d)).wait_send()
-        remote(kvr.at[d], kvr.at[d], k_send.at[d], k_recv.at[d], (g, d)).wait_send()
-        return carry
-
-    lax.fori_loop(0, nt - 1, drain, 0)
 
 
 def put_out(err_ref, kv_ref, attn_ref, err_out, kv_out, attn_out, sem):
@@ -379,12 +380,12 @@
             dma((nx,)),
             dma((nx,)),
             dma((nx,)),
-            dma((nt,)),
-            dma((nt,)),
-            dma((nt,)),
-            dma((nt,)),
-            dma((nt,)),
-            dma((nt,)),
+            dma,
+            dma,
+            dma,
+            dma,
+            dma,
+            dma,
             pltpu.SemaphoreType.REGULAR((8,)),
         ],
         compiler_params=pltpu.CompilerParams(collective_id=0, has_side_effects=True),

time: 35.2 us -> 32.7 us (0.929)
  the two profiles are of different devices: /device:TPU:1 before, /device:TPU:4 now
where the time goes in v4:
time: 32.7 us; the launch traced here: 32.6 us
  Pallas kernels  30.7 us (94%)
  between operations  1.93 us (6%)
    pallas_call x1, Pallas kernels, body(): pl.pallas_call(functools.partial(kernel, (ny, nx, nt, steps)), out_shape=...  30 us
    pallas_call x1, Pallas kernels, body(): pl.pallas_call(put_out, out_shape=tuple((jax.ShapeDtypeStruct(out.shape,...  0.69 us

profile of v4, /device:TPU:4, one launch (start us, length us, event | category | flops | bytes accessed | tf_op | source)
XLA Modules:
  0.0 32.6 jit_solution(672790547353782637)
XLA Ops:
  1.9 30.0 %shard_map.112 = (f32[2,128,128]{2,1,0:T(8,128)S(1)}, bf16[4,128]{1,0:T(4,128)(2,1)S(1)}, bf16[4,512]{1,0:T(4,128)(2,1)S(1)}) custom-call(s32[1,2]{1,0:T(1,128)} %idx_hbm.1, s32[1]{0:T(128)S(6)} %copy.12.tally_hbm, s32[1]{0:T(128)S(6)} %copy.13.fill_hbm, f32[2,128,128]{2,1,0:T(8,128)} %inc_ref.1, f32[2,128,128]{2,1,0:T(8,128)} %res_ref.1, ...), custom_call_target="tpu_custom_call" | custom-call | tf_op jit(solution)/shard_map/pallas_call | solution.py:345
  31.9 0.7 %shard_map.113 = (f32[2,128,128]{2,1,0:T(8,128)}, bf16[4,128]{1,0:T(4,128)(2,1)}, bf16[4,512]{1,0:T(4,128)(2,1)}) custom-call(f32[2,128,128]{2,1,0:T(8,128)S(1)} %get-tuple-element.9.err_ref, bf16[4,128]{1,0:T(4,128)(2,1)S(1)} %get-tuple-element.10.kv_ref, bf16[4,512]{1,0:T(4,128)(2,1)S(1)} %get-tuple-element.11.attn_ref), custom_call_target="tpu_custom_call" | custom-call | tf_op jit(solution)/shard_map/pallas_call | solution.py:404

commit v5 on v4

--- a/solution.py
+++ b/solution.py
@@ -140,18 +140,25 @@
 
     tell(0)
 
-    w_copies = []
-    for k in range(1, ny):
-        copy = remote(
-            wbuf.at[rows], wbuf.at[rows], w_send.at[k], w_recv.at[y], (((y + k) % ny) * nx + h, t)
-        )
-        copy.start()
-        w_copies.append(copy)
+    w_copies = [
+        remote(wbuf.at[rows], wbuf.at[rows], w_send.at[k], w_recv.at[y], (((y + k) % ny) * nx + h, t))
+        for k in range(1, ny)
+    ]
+
+    def send_weights(turn):
+        @pl.when(h % 2 == turn)
+        def _():
+            for copy in w_copies:
+                copy.start()
+
+    send_weights(0)
     x_copies = []
     for k in range(1, nx):
         copy = remote(xbuf.at[h], xbuf.at[h], x_send.at[k], x_recv.at[h], (y * nx + (h + k) % nx, t))
         copy.start()
         x_copies.append(copy)
+
+    learn(len(reach) - 3)
 
     loads[4].wait()
     for n in range(nx * group):
@@ -186,8 +193,8 @@
                 column = jnp.concatenate([top[part], total[part]], axis=0)
                 stats = jnp.where(lane == 2 * n + i, column, stats)
         if batch[0] == 0:
-            learn(len(reach) - 3)
-    learn(len(reach) - 2)
+            send_weights(1)
+            learn(len(reach) - 2)
     square = jnp.concatenate([stats, jnp.zeros((HD - 2 * half, HD), F32)], axis=0)
     flipped = square.T
     for n in range(nt):

time: 32.7 us -> 32.4 us (level)
  the two profiles are of different devices: /device:TPU:4 before, /device:TPU:1 now
where the time goes in v5:
time: 32.4 us; the launch traced here: 31.8 us
  Pallas kernels  29.9 us (92%)
  between operations  1.93 us (6%)
    pallas_call x1, Pallas kernels, body(): pl.pallas_call(functools.partial(kernel, (ny, nx, nt, steps)), out_shape=...  29.2 us
    pallas_call x1, Pallas kernels, body(): pl.pallas_call(put_out, out_shape=tuple((jax.ShapeDtypeStruct(out.shape,...  0.69 us

profile of v5, /device:TPU:1, one launch (start us, length us, event | category | flops | bytes accessed | tf_op | source)
XLA Modules:
  0.0 31.8 jit_solution(9702991593780580112)
XLA Ops:
  1.9 29.2 %shard_map.112 = (f32[2,128,128]{2,1,0:T(8,128)S(1)}, bf16[4,128]{1,0:T(4,128)(2,1)S(1)}, bf16[4,512]{1,0:T(4,128)(2,1)S(1)}) custom-call(s32[1,2]{1,0:T(1,128)} %idx_hbm.1, s32[1]{0:T(128)S(6)} %copy.12.tally_hbm, s32[1]{0:T(128)S(6)} %copy.13.fill_hbm, f32[2,128,128]{2,1,0:T(8,128)} %inc_ref.1, f32[2,128,128]{2,1,0:T(8,128)} %res_ref.1, ...), custom_call_target="tpu_custom_call" | custom-call | tf_op jit(solution)/shard_map/pallas_call | solution.py:352
  31.1 0.7 %shard_map.113 = (f32[2,128,128]{2,1,0:T(8,128)}, bf16[4,128]{1,0:T(4,128)(2,1)}, bf16[4,512]{1,0:T(4,128)(2,1)}) custom-call(f32[2,128,128]{2,1,0:T(8,128)S(1)} %get-tuple-element.9.err_ref, bf16[4,128]{1,0:T(4,128)(2,1)S(1)} %get-tuple-element.10.kv_ref, bf16[4,512]{1,0:T(4,128)(2,1)S(1)} %get-tuple-element.11.attn_ref), custom_call_target="tpu_custom_call" | custom-call | tf_op jit(solution)/shard_map/pallas_call | solution.py:411

commit v6 on v5

--- a/solution.py
+++ b/solution.py
@@ -94,9 +94,6 @@
         pltpu.make_async_copy(tally_hbm, tally_ref, in_sem.at[6]),
         pltpu.make_async_copy(fill_hbm, fill_ref, in_sem.at[7]),
     ]
-    for copy in loads[:4] + loads[5:]:
-        copy.start()
-
     barrier = pltpu.get_barrier_semaphore()
     for k in (1, nt - 1):
         pl.semaphore_signal(barrier, inc=1, device_id=(g, (t + k) % nt), device_id_type=MESH)
@@ -105,13 +102,8 @@
     for k in range(1, ny):
         pl.semaphore_signal(barrier, inc=1, device_id=(((y + k) % ny) * nx + h, t), device_id_type=MESH)
 
-    loads[4].start()
-    cache_loads = []
-    for n in range(nx):
-        cols = slice(n * 2 * HD, (n + 1) * 2 * HD)
-        copy = pltpu.make_async_copy(cache_ref.at[:, cols], cache_v.at[:, cols], cache_sem.at[n])
+    for copy in loads[:4] + loads[5:]:
         copy.start()
-        cache_loads.append(copy)
 
     for copy in loads[:4] + loads[5:]:
         copy.wait()
@@ -157,6 +149,14 @@
         copy = remote(xbuf.at[h], xbuf.at[h], x_send.at[k], x_recv.at[h], (y * nx + (h + k) % nx, t))
         copy.start()
         x_copies.append(copy)
+
+    loads[4].start()
+    cache_loads = []
+    for n in range(nx):
+        cols = slice(n * 2 * HD, (n + 1) * 2 * HD)
+        copy = pltpu.make_async_copy(cache_ref.at[:, cols], cache_v.at[:, cols], cache_sem.at[n])
+        copy.start()
+        cache_loads.append(copy)
 
     learn(len(reach) - 3)
 

time: 32.4 us -> 31.7 us (0.978); the launches traced: 31.8 us -> 31.5 us
  no operation moved by 1% of the time
where the time goes in v6:
time: 31.7 us; the launch traced here: 31.5 us
  Pallas kernels  29.6 us (93%)
  between operations  1.93 us (6%)
    pallas_call x1, Pallas kernels, body(): pl.pallas_call(functools.partial(kernel, (ny, nx, nt, steps)), out_shape=...  28.9 us
    pallas_call x1, Pallas kernels, body(): pl.pallas_call(put_out, out_shape=tuple((jax.ShapeDtypeStruct(out.shape,...  0.69 us

profile of v6, /device:TPU:1, one launch (start us, length us, event | category | flops | bytes accessed | tf_op | source)
XLA Modules:
  0.0 31.5 jit_solution(3417105520631381772)
XLA Ops:
  1.9 28.9 %shard_map.112 = (f32[2,128,128]{2,1,0:T(8,128)S(1)}, bf16[4,128]{1,0:T(4,128)(2,1)S(1)}, bf16[4,512]{1,0:T(4,128)(2,1)S(1)}) custom-call(s32[1,2]{1,0:T(1,128)} %idx_hbm.1, s32[1]{0:T(128)S(6)} %copy.12.tally_hbm, s32[1]{0:T(128)S(6)} %copy.13.fill_hbm, f32[2,128,128]{2,1,0:T(8,128)} %inc_ref.1, f32[2,128,128]{2,1,0:T(8,128)} %res_ref.1, ...), custom_call_target="tpu_custom_call" | custom-call | tf_op jit(solution)/shard_map/pallas_call | solution.py:352
  30.8 0.7 %shard_map.113 = (f32[2,128,128]{2,1,0:T(8,128)}, bf16[4,128]{1,0:T(4,128)(2,1)}, bf16[4,512]{1,0:T(4,128)(2,1)}) custom-call(f32[2,128,128]{2,1,0:T(8,128)S(1)} %get-tuple-element.9.err_ref, bf16[4,128]{1,0:T(4,128)(2,1)S(1)} %get-tuple-element.10.kv_ref, bf16[4,512]{1,0:T(4,128)(2,1)S(1)} %get-tuple-element.11.attn_ref), custom_call_target="tpu_custom_call" | custom-call | tf_op jit(solution)/shard_map/pallas_call | solution.py:411
